TPU v7x, 512 devices: a whole 4x4x16 slice. The times are simulated.
512 devices in a mesh: dp: 64 (over z, x), seq: 8 (over y, core).
Axes of the slice: x: 4, y: 4, z: 16, core: 2. Of those that a mesh axis runs over, the one named last changes fastest.
Arguments:
- acts: bfloat16 [65536, 4096], P('dp', 'seq'), may hold values from -6 to 6
- upstream: bfloat16 [65536, 1024], P(('dp', 'seq')), may hold values from -0.005859375 to 0.005859375
- keep_lists: int32 [64, 8], replicated, may hold values from 0 to 15, all different within a row
- left_gram: float32 [8, 64, 1, 64, 64], P('seq', 'dp'), as said below
- right_gram: float32 [8, 64, 1, 64, 64], P('seq', 'dp'), as said below
- left_basis: float32 [8, 64, 1, 64, 64], P('seq', 'dp'), may hold values from -0.75 to 0.75
- right_basis: float32 [8, 64, 1, 64, 64], P('seq', 'dp'), may hold values from -0.75 to 0.75
- second_moment: float32 [8, 64, 1, 64, 64], P('seq', 'dp'), may hold values from 0.004 to 0.04
Outputs:
- new_left: float32 [8, 64, 1, 64, 64], P('seq', 'dp')
- new_right: float32 [8, 64, 1, 64, 64], P('seq', 'dp')
- direction: float32 [8, 64, 1, 64, 64], P('seq', 'dp')
Inputs may be any that keep to these rules, and one draw needn't show every extreme that they name: `keep_lists`: each row lists 8 different column blocks, and every column block is kept in some row. `left_gram`: each block is symmetric. `right_gram`: each block is symmetric.
All inputs are finite; a program needn't handle non-finite values.
Results may differ from a plain program's by a relative error of at most 0.0003.
Values may be sent and summed in bfloat16 or wider, within the bound.
No kernel may reach another device: no remote copies, remote signals or barrier semaphores. Data moves between devices by JAX's collectives and lax.ppermute only.
A program may use at most 64 MiB of HBM per device.

v0:
```python
import jax
import jax.numpy as jnp
from jax import lax
from jax.sharding import PartitionSpec as P

BLOCK = 64


def precondition(gradient, left_gram, right_gram, left_basis, right_basis, second_moment):
    highest = lax.Precision.HIGHEST
    new_left = 0.95 * left_gram + 0.05 * jnp.einsum(
        "...ij,...kj->...ik", gradient, gradient, precision=highest
    )
    new_right = 0.95 * right_gram + 0.05 * jnp.einsum(
        "...ji,...jk->...ik", gradient, gradient, precision=highest
    )
    partial_rot = jnp.einsum("...ji,...jk->...ik", left_basis, gradient, precision=highest)
    rotated = jnp.einsum("...ij,...jk->...ik", partial_rot, right_basis, precision=highest)
    second = 0.95 * second_moment + 0.05 * rotated * rotated
    scaled = rotated / (jnp.sqrt(second) + 1e-08)
    partial_back = jnp.einsum("...ij,...jk->...ik", left_basis, scaled, precision=highest)
    direction = jnp.einsum("...ij,...kj->...ik", partial_back, right_basis, precision=highest)
    return (new_left, new_right, direction)


def per_device(
    acts, upstream, keep_lists, left_gram, right_gram, left_basis, right_basis, second_moment
):
    share_rows = acts.shape[1]
    share_blocks = share_rows // BLOCK
    kept_share = lax.dynamic_slice_in_dim(
        keep_lists, lax.axis_index("seq") * share_blocks, share_blocks, 0
    )
    gathered = lax.all_gather(upstream, "seq", axis=0, tiled=True)
    grad = lax.dot_general(
        acts, gathered, (((0,), (0,)), ((), ())), preferred_element_type=jnp.float32
    )
    tiles = grad.reshape(share_blocks, BLOCK, grad.shape[1] // BLOCK, BLOCK)
    picked = jnp.take_along_axis(tiles, kept_share[:, None, :, None], axis=2)
    packed = picked.transpose(0, 2, 1, 3)
    data_size = lax.axis_size("dp")
    outgoing = packed.reshape(data_size, -1, BLOCK * BLOCK)
    arrived = lax.all_to_all(outgoing, "dp", split_axis=0, concat_axis=0, tiled=True)
    owned_sum = jnp.sum(arrived, axis=0)
    gradient = owned_sum.reshape(1, 1, -1, BLOCK, BLOCK)
    new_left, new_right, direction = precondition(
        gradient, left_gram, right_gram, left_basis, right_basis, second_moment
    )
    return (new_left, new_right, direction)


def solution(mesh):
    in_specs = (
        P("dp", "seq"),
        P(("dp", "seq"), None),
        P(),
        P("seq", "dp", None, None, None),
        P("seq", "dp", None, None, None),
        P("seq", "dp", None, None, None),
        P("seq", "dp", None, None, None),
        P("seq", "dp", None, None, None),
    )
    out_specs = (
        P("seq", "dp", None, None, None),
        P("seq", "dp", None, None, None),
        P("seq", "dp", None, None, None),
    )
    return jax.shard_map(
        per_device, mesh=mesh, in_specs=in_specs, out_specs=out_specs, check_vma=False
    )
```

profile of v0, /device:TPU:2, one launch (start us, length us, event | category | flops | bytes accessed | tf_op | source)
XLA Modules:
  0.0 149.2 jit_solution(2693960995745928037)
XLA Ops:
  7.2 0.0 copy-start
  7.2 0.0 all-gather.2.cloned.1.call-start
  7.2 0.7 all-gather.2.cloned.1.call-update
  7.9 0.8 constant_dynamic-slice_fusion
  8.7 0.1 copy.17
  8.8 0.1 reshape.80
  8.9 38.8 %all-gather.2.cloned.1.call-done = bf16[1024,1024]{1,0:T(8,128)(2,1)} async-done(((bf16[128,1024]{1,0:T(8,128)(2,1)}), bf16[1024,1024]{1,0:T(8,128)(2,1)}) %all-gather.2.cloned.1.call-update) | async-done | bytes 2097168 | tf_op jit(solution)/shard_map/all_gather | solution.py:34
  47.6 0.0 copy-done
  47.6 2.9 %fusion.26 = f32[512,1024]{1,0:T(8,128)S(1)} fusion(bf16[1024,512]{1,0:T(8,128)(2,1)S(1)} %copy-done, bf16[1024,1024]{1,0:T(8,128)(2,1)} %all-gather.2.cloned.1.call-done), kind=kOutput, calls=%fused_computation.35 | convolution fusion | flops 1073741824 | bytes 5242880 | tf_op jit(solution)/shard_map/dot_general | solution.py:35
  50.5 2.6 %reshape.73 = f32[8,64,16,64]{3,2,1,0:T(8,128)} reshape(f32[512,1024]{1,0:T(8,128)S(1)} %fusion.26) | data formatting | bytes 4194304 | tf_op jit(solution)/shard_map/reshape | solution.py:38
  53.0 5.4 %copy.15 = f32[8,64,16,64]{3,1,2,0:T(8,128)} copy(f32[8,64,16,64]{3,2,1,0:T(8,128)} %reshape.73) | data formatting | bytes 4194304 | tf_op jit(solution)/shard_map/reshape | solution.py:38
  58.4 4.2 %gather_fusion = f32[64,64,64]{2,1,0:T(8,128)} fusion(f32[8,64,16,64]{3,1,2,0:T(8,128)} %copy.15, s32[64]{0:T(128)S(1)} %reshape.80), kind=kCustom, calls=%fused_computation | custom fusion | bytes 2097664 | tf_op jit(solution)/shard_map/jit(take_along_axis)/gather | solution.py:39
  62.6 1.8 %broadcast_select_fusion = f32[8,8,64,64]{3,2,1,0:T(8,128)S(1)} fusion(f32[8,8,64,64]{3,2,1,0:T(8,128)} %bitcast.57, pred[8,8]{1,0:T(8,128)(4,1)S(1)} %compare_and_fusion), kind=kLoop, calls=%fused_computation.8 | loop fusion | flops 262144 | bytes 2097216 | tf_op jit(solution)/shard_map/jit(take_along_axis)/select_n | solution.py:39
  64.4 2.3 %reshape.91 = f32[64,1,4096]{2,1,0:T(1,128)} reshape(f32[8,8,64,64]{3,2,1,0:T(8,128)S(1)} %broadcast_select_fusion) | data formatting | bytes 2097152 | tf_op jit(solution)/shard_map/reshape | solution.py:42
  66.7 0.0 copy-start.3
  66.7 0.0 copy-start.4
  66.7 0.0 copy-start.2
  66.7 0.0 copy-start.1
  66.7 0.0 copy-start.5
  66.7 71.4 %all_to_all.5 = f32[64,1,4096]{2,1,0:T(1,128)S(1)} all-to-all(f32[64,1,4096]{2,1,0:T(1,128)} %reshape.91), channel_id=1, replica_groups=mesh['dp'=64,'seq'=8] {'dp'}, dimensions={0} | all-to-all | bytes 2097152 | tf_op jit(solution)/shard_map/all_to_all | solution.py:43
  138.1 0.9 reduce_sum.9
  139.0 0.1 reshape.76
  139.1 0.0 copy-done.3
  139.1 0.8 fusion.2
  139.9 0.0 copy-done.4
  139.9 0.9 fusion.3
  140.7 0.0 copy-done.2
  140.7 0.2 fusion.17
  141.0 0.0 copy-done.1
  141.0 0.2 fusion.14
  141.2 0.0 copy-done.5
  141.2 0.3 fusion.10
  141.5 0.9 convolution_bitcast_fusion
  (2 shorter events, 0.0 us)
Async XLA Ops:
  7.2 40.5 %copy-start = (bf16[1024,512]{1,0:T(8,128)(2,1)S(1)}, bf16[1024,512]{1,0:T(8,128)(2,1)}, u32[]{:S(2)}) copy-start(bf16[1024,512]{1,0:T(8,128)(2,1)} %param.8) | copy-start | bytes 3145732
  7.2 40.4 %all-gather.2.cloned.1.call-start = ((), (), s32[]{:S(2)}) async-start(), calls=%async_computation.1 | async-start | bytes 2359296 | tf_op jit(solution)/shard_map/all_gather | solution.py:34
  66.7 72.4 %copy-start.3 = (f32[1,1,1,64,64]{4,3,2,1,0:T(8,128)S(1)}, f32[1,1,1,64,64]{4,3,2,1,0:T(8,128)}, u32[]{:S(2)}) copy-start(f32[1,1,1,64,64]{4,3,2,1,0:T(8,128)} %param.11) | copy-start | bytes 49156
  66.7 73.2 %copy-start.4 = (f32[1,1,1,64,64]{4,3,2,1,0:T(8,128)S(1)}, f32[1,1,1,64,64]{4,3,2,1,0:T(8,128)}, u32[]{:S(2)}) copy-start(f32[1,1,1,64,64]{4,3,2,1,0:T(8,128)} %param.12) | copy-start | bytes 49156
  66.7 74.0 %copy-start.2 = (f32[1,1,1,64,64]{4,3,2,1,0:T(8,128)S(1)}, f32[1,1,1,64,64]{4,3,2,1,0:T(8,128)}, u32[]{:S(2)}) copy-start(f32[1,1,1,64,64]{4,3,2,1,0:T(8,128)} %param.13) | copy-start | bytes 49156
  66.7 74.3 %copy-start.1 = (f32[1,1,1,64,64]{4,3,2,1,0:T(8,128)S(1)}, f32[1,1,1,64,64]{4,3,2,1,0:T(8,128)}, u32[]{:S(2)}) copy-start(f32[1,1,1,64,64]{4,3,2,1,0:T(8,128)} %param.14) | copy-start | bytes 49156
  66.7 74.5 %copy-start.5 = (f32[1,1,1,64,64]{4,3,2,1,0:T(8,128)S(1)}, f32[1,1,1,64,64]{4,3,2,1,0:T(8,128)}, u32[]{:S(2)}) copy-start(f32[1,1,1,64,64]{4,3,2,1,0:T(8,128)} %param.15) | copy-start | bytes 49156
Sparse Core Ops, SparseCore 0:
  10.1 37.4 all-gather.1
where the time goes:
time: 150 us; the launch traced here: 149 us
  blocking collectives  71.4 us (48%)
  waiting for transfers between devices  39.4 us (26%)
  local copies, waits for them, and re-layouts  15.4 us (10%)
  between operations  14.1 us (9%)
  matrix products  6.08 us (4%)
  other arithmetic  2.68 us (2%)
    all_to_all x1, blocking collectives, per_device(): lax.all_to_all(outgoing, 'dp', split_axis=0, concat_axis=0, tiled=True)  71.4 us
    all_gather x1, waiting for transfers between devices, per_device(): gathered = lax.all_gather(upstream, 'seq', axis=0, tiled=True)  38.8 us
    reshape x2, local copies, waits for them, and re-layouts, per_device(): tiles = grad.reshape(share_blocks, BLOCK, grad.shape[1] // BLOCK, BLOCK)  7.94 us
    gather x2, local copies, waits for them, and re-layouts, per_device(): picked = jnp.take_along_axis(tiles, kept_share[:, None, :, None], axis=2)  4.28 us
  transfers between devices with their start and end apart: 1, of which 1 were waited for; matrix products, arithmetic and copies ran while one was open for 1% of the time, Pallas kernels for 0%

commit v1 on v0

--- a/solution.py
+++ b/solution.py
@@ -31,7 +31,9 @@
     kept_share = lax.dynamic_slice_in_dim(
         keep_lists, lax.axis_index("seq") * share_blocks, share_blocks, 0
     )
-    gathered = lax.all_gather(upstream, "seq", axis=0, tiled=True)
+    gathered = jnp.concatenate(
+        lax.all_to_all(jnp.stack([upstream] * lax.axis_size("seq")), "seq", 0, 0), axis=0
+    )
     grad = lax.dot_general(
         acts, gathered, (((0,), (0,)), ((), ())), preferred_element_type=jnp.float32
     )

time: 150 us -> 130 us (0.87)
  waiting for transfers between devices: 39.4 us -> 25.6 us
  between operations: 14.1 us -> 0.77 us
  starting transfers between devices: 0.04 us -> 4.6 us
  blocking collectives: 71.4 us -> 73.4 us
    all_gather x1 -> x0, waiting for transfers between devices: 38.8 us -> none  [per_device(): gathered = lax.all_gather(upstream, 'seq', axis=0, tiled=True)]
    all_to_all x0 -> x1, waiting for transfers between devices: none -> 25.6 us  [per_device(): lax.all_to_all(jnp.stack([upstream] * lax.axis_size('seq')), 'seq', 0, 0)]
    reshape x2 -> x0, local copies, waits for them, and re-layouts: 7.94 us -> none  [per_device(): tiles = grad.reshape(share_blocks, BLOCK, grad.shape[1] // BLOCK, BLOCK)]
    all_to_all x0 -> x1, starting transfers between devices: none -> 4.6 us  [per_device(): lax.all_to_all(jnp.stack([upstream] * lax.axis_size('seq')), 'seq', 0, 0)]
    dot_general x0 -> x1, local copies, waits for them, and re-layouts: none -> 2.94 us  [per_device(): lax.dot_general(acts, gathered, (((0,), (0,)), ((), ())), preferred_eleme...]
    all_to_all x0 -> x1, local copies, waits for them, and re-layouts: none -> 2.59 us  [per_device(): lax.all_to_all(jnp.stack([upstream] * lax.axis_size('seq')), 'seq', 0, 0)]
    unnamed x13 -> x19, local copies, waits for them, and re-layouts: 0.1 us -> 2.57 us
    all_to_all x1, blocking collectives: 71.4 us -> 73.4 us  [per_device(): lax.all_to_all(outgoing, 'dp', split_axis=0, concat_axis=0, tiled=True)]
where the time goes in v1:
time: 130 us
  blocking collectives  73.4 us (56%)
  waiting for transfers between devices  25.6 us (20%)
  local copies, waits for them, and re-layouts  15.5 us (12%)
  matrix products  7.17 us (6%)
  starting transfers between devices  4.6 us (4%)
  other arithmetic  2.68 us (2%)
    all_to_all x1, blocking collectives, per_device(): lax.all_to_all(outgoing, 'dp', split_axis=0, concat_axis=0, tiled=True)  73.4 us
    all_to_all x1, waiting for transfers between devices, per_device(): lax.all_to_all(jnp.stack([upstream] * lax.axis_size('seq')), 'seq', 0, 0)  25.6 us
    all_to_all x1, starting transfers between devices, per_device(): lax.all_to_all(jnp.stack([upstream] * lax.axis_size('seq')), 'seq', 0, 0)  4.6 us
    gather x2, local copies, waits for them, and re-layouts, per_device(): picked = jnp.take_along_axis(tiles, kept_share[:, None, :, None], axis=2)  4.3 us
    dot_general x1, matrix products, per_device(): lax.dot_general(acts, gathered, (((0,), (0,)), ((), ())), preferred_eleme...  3.94 us
    dot_general x1, local copies, waits for them, and re-layouts, per_device(): lax.dot_general(acts, gathered, (((0,), (0,)), ((), ())), preferred_eleme...  2.94 us
  transfers between devices with their start and end apart: 1, of which 1 were waited for; matrix products, arithmetic and copies ran while one was open for 1% of the time, Pallas kernels for 0%

profile of v1, /device:TPU:2, one launch (start us, length us, event | category | flops | bytes accessed | tf_op | source)
XLA Modules:
  0.0 129.7 jit_solution(8108660636090348208)
XLA Ops:
  0.6 0.0 copy-start
  0.6 1.1 copy.22
  1.8 1.6 %stack.2 = bf16[8,128,1024]{1,2,0:T(8,128)(2,1)} broadcast(bf16[128,1024]{0,1:T(8,128)(2,1)S(1)} %copy.22), dimensions={1,2} | broadcast | bytes 2359296 | tf_op jit(solution)/shard_map/stack | solution.py:35
  3.4 0.0 copy-start.1
  3.4 4.6 %all-to-all-start = ((bf16[8,128,1024]{1,2,0:T(8,128)(2,1)}), bf16[8,128,1024]{1,2,0:T(8,128)(2,1)S(1)}, u32[]{:S(2)}, u32[]{:S(2)}) async-start(bf16[8,128,1024]{1,2,0:T(8,128)(2,1)} %stack.2), calls=%async_computation | async-start | bytes 4194304 | tf_op jit(solution)/shard_map/all_to_all | solution.py:35
  8.0 0.0 copy-start.6
  8.0 0.0 copy-done.1
  8.0 1.3 %copy.21 = bf16[1024,512]{0,1:T(8,128)(2,1)} copy(bf16[1024,512]{1,0:T(8,128)(2,1)S(1)} %copy-done.1) | data formatting | bytes 2097152 | tf_op args[0]
  9.4 0.0 copy-done.6
  9.4 0.1 constant_dynamic-slice_fusion
  9.4 0.1 copy.26
  9.5 0.1 reshape.85
  9.6 25.6 %all-to-all-done = bf16[8,128,1024]{1,2,0:T(8,128)(2,1)S(1)} async-done(((bf16[8,128,1024]{1,2,0:T(8,128)(2,1)}), bf16[8,128,1024]{1,2,0:T(8,128)(2,1)S(1)}, u32[]{:S(2)}, u32[]{:S(2)}) %all-to-all-start) | async-done | bytes 2097184 | tf_op jit(solution)/shard_map/all_to_all | solution.py:35
  35.2 2.6 %copy.23 = bf16[8,128,1024]{2,1,0:T(8,128)(2,1)} copy(bf16[8,128,1024]{1,2,0:T(8,128)(2,1)S(1)} %all-to-all-done) | data formatting | bytes 4194304 | tf_op jit(solution)/shard_map/all_to_all | solution.py:35
  37.8 0.0 copy-start.2
  37.8 2.9 %copy.24 = bf16[1024,1024]{1,0:T(8,128)(2,1)S(1)} copy(bf16[1024,1024]{0,1:T(8,128)(2,1)} %bitcast.71) | data formatting | bytes 4194304 | tf_op jit(solution)/shard_map/dot_general | solution.py:37
  40.7 0.0 copy-done.2
  40.7 3.9 %fusion.26 = f32[8,64,16,64]{3,1,2,0:T(8,128)} fusion(bf16[8,64,1024,1]{2,1,3,0:T(8,128)(2,1)S(1)} %bitcast.73, bf16[16,64,1024,1]{2,1,0,3:T(8,128)(2,1)S(1)} %bitcast.72), kind=kOutput, calls=%fused_computation.35 | convolution fusion | flops 1073741824 | bytes 5242880 | tf_op jit(solution)/shard_map/dot_general | solution.py:37
  44.7 4.2 %gather_fusion = f32[64,64,64]{2,1,0:T(8,128)} fusion(f32[8,64,16,64]{3,1,2,0:T(8,128)} %fusion.26, s32[64]{0:T(128)S(1)} %reshape.85), kind=kCustom, calls=%fused_computation | custom fusion | bytes 2097664 | tf_op jit(solution)/shard_map/jit(take_along_axis)/gather | solution.py:41
  48.9 1.8 %broadcast_select_fusion = f32[8,8,64,64]{3,2,1,0:T(8,128)S(1)} fusion(f32[8,8,64,64]{3,2,1,0:T(8,128)} %bitcast.70, pred[8,8]{1,0:T(8,128)(4,1)S(1)} %compare_and_fusion), kind=kLoop, calls=%fused_computation.8 | loop fusion | flops 262144 | bytes 2097216 | tf_op jit(solution)/shard_map/jit(take_along_axis)/select_n | solution.py:41
  50.7 1.3 reshape.80
  52.0 0.0 copy-start.4
  52.0 0.0 copy-start.5
  52.0 0.0 copy-start.3
  52.0 0.0 copy-start.7
  52.0 73.4 %all_to_all.10 = f32[64,1,4096]{2,1,0:T(1,128)S(1)} all-to-all(f32[64,1,4096]{2,1,0:T(1,128)S(1)} %reshape.80), channel_id=1, replica_groups=mesh['dp'=64,'seq'=8] {'dp'}, dimensions={0} | all-to-all | bytes 2097152 | tf_op jit(solution)/shard_map/all_to_all | solution.py:45
  125.5 0.9 reduce_sum.9
  126.3 0.1 reshape.81
  126.4 0.0 copy-done.4
  126.4 0.8 fusion.2
  127.2 0.0 copy-done.5
  127.2 0.9 fusion.3
  128.1 0.0 copy-done
  128.1 0.2 fusion.17
  128.3 0.0 copy-done.3
  128.3 0.2 fusion.14
  128.6 0.0 copy-done.7
  128.6 0.3 fusion.10
  128.8 0.8 convolution_bitcast_fusion
  (2 shorter events, 0.0 us)
Async XLA Ops:
  0.6 127.5 %copy-start = (f32[1,1,1,64,64]{4,3,2,1,0:T(8,128)S(1)}, f32[1,1,1,64,64]{4,3,2,1,0:T(8,128)}, u32[]{:S(2)}) copy-start(f32[1,1,1,64,64]{4,3,2,1,0:T(8,128)} %param.13) | copy-start | bytes 49156
  3.4 4.6 %copy-start.1 = (bf16[1024,512]{1,0:T(8,128)(2,1)S(1)}, bf16[1024,512]{1,0:T(8,128)(2,1)}, u32[]{:S(2)}) copy-start(bf16[1024,512]{1,0:T(8,128)(2,1)} %param.8) | copy-start | bytes 3145732
  3.4 31.8 %all-to-all-start = ((bf16[8,128,1024]{1,2,0:T(8,128)(2,1)}), bf16[8,128,1024]{1,2,0:T(8,128)(2,1)S(1)}, u32[]{:S(2)}, u32[]{:S(2)}) async-start(bf16[8,128,1024]{1,2,0:T(8,128)(2,1)} %stack.2), calls=%async_computation | async-start | bytes 4194304 | tf_op jit(solution)/shard_map/all_to_all | solution.py:35
  8.0 1.3 %copy-start.6 = (s32[64,8]{0,1:T(8,128)S(1)}, s32[64,8]{0,1:T(8,128)}, u32[]{:S(2)}) copy-start(s32[64,8]{0,1:T(8,128)} %param.10) | copy-start | bytes 6148
  37.8 3.0 %copy-start.2 = (bf16[1024,512]{0,1:T(8,128)(2,1)S(1)}, bf16[1024,512]{0,1:T(8,128)(2,1)}, u32[]{:S(2)}) copy-start(bf16[1024,512]{0,1:T(8,128)(2,1)} %copy.21) | copy-start | bytes 3145732
  52.0 74.4 %copy-start.4 = (f32[1,1,1,64,64]{4,3,2,1,0:T(8,128)S(1)}, f32[1,1,1,64,64]{4,3,2,1,0:T(8,128)}, u32[]{:S(2)}) copy-start(f32[1,1,1,64,64]{4,3,2,1,0:T(8,128)} %param.11) | copy-start | bytes 49156
  52.0 75.2 %copy-start.5 = (f32[1,1,1,64,64]{4,3,2,1,0:T(8,128)S(1)}, f32[1,1,1,64,64]{4,3,2,1,0:T(8,128)}, u32[]{:S(2)}) copy-start(f32[1,1,1,64,64]{4,3,2,1,0:T(8,128)} %param.12) | copy-start | bytes 49156
  52.0 76.3 %copy-start.3 = (f32[1,1,1,64,64]{4,3,2,1,0:T(8,128)S(1)}, f32[1,1,1,64,64]{4,3,2,1,0:T(8,128)}, u32[]{:S(2)}) copy-start(f32[1,1,1,64,64]{4,3,2,1,0:T(8,128)} %param.14) | copy-start | bytes 49156
  52.0 76.6 %copy-start.7 = (f32[1,1,1,64,64]{4,3,2,1,0:T(8,128)S(1)}, f32[1,1,1,64,64]{4,3,2,1,0:T(8,128)}, u32[]{:S(2)}) copy-start(f32[1,1,1,64,64]{4,3,2,1,0:T(8,128)} %param.15) | copy-start | bytes 49156
